TPU v7x, 32 devices: a whole 2x2x4 slice. The times are simulated.
32 devices in a mesh: lon: 8 (over z, x), lat: 4 (over y, core).
Axes of the slice: x: 2, y: 2, z: 4, core: 2. Of those that a mesh axis runs over, the one named last changes fastest.
Arguments:
- field: float32 [2, 128, 512], P(None, 'lat', 'lon'), may hold values from -6 to 6
- gamma: float32 [2, 128, 512], P(None, 'lat', 'lon'), may hold values from 1 to 192
- kappa_zonal: float32 [2, 128, 512], P(None, 'lat', 'lon'), may hold values from 4096 to 49152
- kappa_merid: float32 [2, 128, 512], P(None, 'lat', 'lon'), may hold values from 1024 to 12288
- area: float32 [128, 512], P('lat', 'lon'), may hold values from 0.3 to 3
- sea_mask: int32 [128, 512], P('lat', 'lon'), may hold values from 0 to 1, as said below
- fold_pair: int32 [512], P('lon'), may hold values from 0 to 511, as said below
Outputs:
- covaried: float32 [2, 128, 512], P(None, 'lat', 'lon')
Inputs may be any that keep to these rules, and one draw needn't show every extreme that they name: `sea_mask`: ocean cells are 1 and land cells 0; land comes in rectangles, periodic in longitude. A mirror pairing across the fold: fold_pair[i] + i is the same odd number modulo 512 for every i, so fold_pair[fold_pair[i]] == i and fold_pair[i] != i.
All inputs are finite; a program needn't handle non-finite values.
Results may differ from a plain program's by a relative error of at most 0.00095.
Values sent between devices are 32-bit elements; how exact they have to be, the bound alone decides.
No kernel may reach another device: no remote copies, remote signals or barrier semaphores. Data moves between devices by JAX's collectives and lax.ppermute only.
A program may use at most 64 MiB of HBM per device.

v0:
```python
import jax
import jax.numpy as jnp
from jax import lax
from jax.sharding import PartitionSpec as P


def passed_along(block, axis, distance):
    devices = range(lax.axis_size(axis))
    route = [((i - distance) % len(devices), i) for i in devices]
    return lax.ppermute(block, axis, route)


def passed_along_2(value, axis, by):
    size = lax.axis_size(axis)
    pairs = [(i, i + by) for i in range(size) if 0 <= i + by < size]
    return lax.ppermute(value, axis, pairs)


def slide(values, offset, fill, wrap):
    if wrap:
        return jnp.roll(values, offset, axis=-1)
    edge = jnp.full(values.shape[:-1] + (abs(offset),), fill, values.dtype)
    if offset > 0:
        return jnp.concatenate([edge, values[..., :-offset]], axis=-1)
    return jnp.concatenate([values[..., -offset:], edge], axis=-1)


def reduce_lines(lower, diagonal, upper, source, wrap):
    length = source.shape[-1]
    stride = 1
    while stride < length:
        below_diag = slide(diagonal, stride, 1.0, wrap)
        above_diag = slide(diagonal, -stride, 1.0, wrap)
        factor_low = -lower / below_diag
        factor_up = -upper / above_diag
        new_diagonal = (
            diagonal
            + factor_low * slide(upper, stride, 0.0, wrap)
            + factor_up * slide(lower, -stride, 0.0, wrap)
        )
        source = (
            source
            + factor_low * slide(source, stride, 0.0, wrap)
            + factor_up * slide(source, -stride, 0.0, wrap)
        )
        lower = factor_low * slide(lower, stride, 0.0, wrap)
        upper = factor_up * slide(upper, -stride, 0.0, wrap)
        diagonal = new_diagonal
        stride = stride * 2
    if wrap:
        return source / (diagonal + lower + upper)
    return source / diagonal


def cyclic_solve(faces, source):
    before = jnp.roll(faces, 1, axis=-1)
    diagonal = 1.0 + before + faces
    return reduce_lines(-before, diagonal, -faces, source, True)


def open_solve(faces, source):
    before = jnp.concatenate([jnp.zeros_like(faces[..., :1]), faces[..., :-1]], axis=-1)
    diagonal = 1.0 + before + faces
    upper_band = jnp.concatenate([-faces[..., :-1], jnp.zeros_like(faces[..., :1])], axis=-1)
    return reduce_lines(-before, diagonal, upper_band, source, False)


def to_columns(blocks, lanes):
    levels, height, breadth = blocks.shape
    split = blocks.reshape(levels, height, lanes, breadth // lanes)
    return jnp.transpose(split, (2, 0, 3, 1))


def from_columns(pieces):
    lanes, levels, narrow, height = pieces.shape
    return jnp.transpose(pieces, (1, 3, 0, 2)).reshape(levels, height, lanes * narrow)


def local(field, gamma, kappa_zonal, kappa_merid, area, sea_mask, fold_pair):
    ocean_cells = sea_mask.astype(jnp.float32)
    east_edge = passed_along(ocean_cells[:, :1], "lon", -1)
    north_edge = passed_along_2(ocean_cells[:1, :], "lat", -1)
    east_ocean = jnp.concatenate([ocean_cells[:, 1:], east_edge], axis=1)
    north_ocean = jnp.concatenate([ocean_cells[1:], north_edge], axis=0)
    zonal_faces = kappa_zonal * (ocean_cells * east_ocean)[None]
    merid_faces = kappa_merid * (ocean_cells * north_ocean)[None]
    scaled = gamma * ocean_cells[None]
    lanes = lax.axis_size("lat")
    zonal_lines = lax.all_to_all(zonal_faces, "lon", split_axis=1, concat_axis=2, tiled=True)
    merid_lines = lax.all_to_all(
        to_columns(merid_faces, lanes), "lat", split_axis=0, concat_axis=3, tiled=True
    )[0]

    def zonal_pass(current):
        lines = lax.all_to_all(current, "lon", split_axis=1, concat_axis=2, tiled=True)
        return lax.all_to_all(
            cyclic_solve(zonal_lines, lines), "lon", split_axis=2, concat_axis=1, tiled=True
        )

    def merid_open(current):
        return lax.all_to_all(
            to_columns(current, lanes), "lat", split_axis=0, concat_axis=3, tiled=True
        )[0]

    def merid_close(columns):
        return from_columns(
            lax.all_to_all(columns[None], "lat", split_axis=3, concat_axis=0, tiled=True)
        )

    current = zonal_pass(scaled * field)
    columns = open_solve(merid_lines, merid_open(current))
    current = merid_close(columns)
    is_top = lax.axis_index("lat") == lanes - 1

    def fold_natural(values):
        top_cells = values[:, -1, :]
        whole_row = lax.all_gather(top_cells, "lon", axis=1, tiled=True)
        partner = jnp.take(whole_row, fold_pair, axis=1)
        return values.at[:, -1, :].set(jnp.where(is_top, 0.5 * (top_cells + partner), top_cells))

    current = fold_natural(current)
    current = current / area[None]
    current = fold_natural(current)
    current = merid_close(open_solve(merid_lines, merid_open(current)))
    current = zonal_pass(current)
    return scaled * current


def solution(mesh):
    return jax.shard_map(
        local,
        mesh=mesh,
        in_specs=(
            P(None, "lat", "lon"),
            P(None, "lat", "lon"),
            P(None, "lat", "lon"),
            P(None, "lat", "lon"),
            P("lat", "lon"),
            P("lat", "lon"),
            P("lon"),
        ),
        out_specs=P(None, "lat", "lon"),
        check_vma=False,
    )
```

profile of v0, /device:TPU:0, one launch (start us, length us, event | category | flops | bytes accessed | tf_op | source)
XLA Modules:
  0.0 188.0 jit_solution(8956095462419415965)
XLA Ops:
  0.7 1.4 collective-permute-start.1
  2.1 6.0 %collective-permute-start = (f32[32,1]{1,0:T(8,128)S(1)}, f32[32,1]{1,0:T(8,128)S(1)}, u32[]{:S(2)}, u32[]{:S(2)}) collective-permute-start(f32[32,1]{1,0:T(8,128)S(1)} %bitcast.116), channel_id=1, source_target_pairs={{4,0},{8,4},{12,8},{16,12},{20,16},{24,20},{28,24},{0,28},{5,1},{9... | collective-permute-start | bytes 392 | tf_op jit(solution)/shard_map/ppermute | solution.py:10
  11.4 3.5 %all-to-all-start.4 = ((f32[4,1,1024]{2,1,0:T(1,128)}), f32[4,1,1024]{2,1,0:T(1,128)S(1)}, u32[]{:S(2)}, u32[]{:S(2)}) async-start(f32[4,1,1024]{2,1,0:T(1,128)} %reshape.120), calls=%async_computation.4 | async-start | bytes 32768 | tf_op jit(solution)/shard_map/all_to_all | solution.py:90
  15.7 3.1 %all-to-all-done.4 = f32[4,1,1024]{2,1,0:T(1,128)S(1)} async-done(((f32[4,1,1024]{2,1,0:T(1,128)}), f32[4,1,1024]{2,1,0:T(1,128)S(1)}, u32[]{:S(2)}, u32[]{:S(2)}) %all-to-all-start.4) | async-done | bytes 16416 | tf_op jit(solution)/shard_map/all_to_all | solution.py:90
  18.8 5.4 %all-to-all-start = ((f32[8,1,512]{2,1,0:T(1,128)}), f32[8,1,512]{2,1,0:T(1,128)S(1)}, u32[]{:S(2)}, u32[]{:S(2)}) async-start(f32[8,1,512]{2,1,0:T(1,128)} %reshape.122), calls=%async_computation | async-start | bytes 32768 | tf_op jit(solution)/shard_map/all_to_all | solution.py:95
  25.8 4.9 %all-to-all-done = f32[8,1,512]{2,1,0:T(1,128)S(1)} async-done(((f32[8,1,512]{2,1,0:T(1,128)}), f32[8,1,512]{2,1,0:T(1,128)S(1)}, u32[]{:S(2)}, u32[]{:S(2)}) %all-to-all-start) | async-done | bytes 16416 | tf_op jit(solution)/shard_map/all_to_all | solution.py:95
  30.8 3.3 %all-to-all-start.1 = ((f32[8,1,512]{2,1,0:T(1,128)}), f32[8,1,512]{2,1,0:T(1,128)S(1)}, u32[]{:S(2)}, u32[]{:S(2)}) async-start(f32[8,1,512]{2,1,0:T(1,128)} %reshape.124), calls=%async_computation.1 | async-start | bytes 32768 | tf_op jit(solution)/shard_map/all_to_all | solution.py:89
  35.2 5.4 %all-to-all-done.1 = f32[8,1,512]{2,1,0:T(1,128)S(1)} async-done(((f32[8,1,512]{2,1,0:T(1,128)}), f32[8,1,512]{2,1,0:T(1,128)S(1)}, u32[]{:S(2)}, u32[]{:S(2)}) %all-to-all-start.1) | async-done | bytes 16416 | tf_op jit(solution)/shard_map/all_to_all | solution.py:89
  48.2 1.3 reshape.126
  49.5 3.3 %all-to-all-start.2 = ((f32[8,1,512]{2,1,0:T(1,128)}), f32[8,1,512]{2,1,0:T(1,128)S(1)}, u32[]{:S(2)}, u32[]{:S(2)}) async-start(f32[8,1,512]{2,1,0:T(1,128)} %reshape.126), calls=%async_computation.2 | async-start | bytes 32768 | tf_op jit(solution)/shard_map/all_to_all | solution.py:96
  52.9 6.4 %all-to-all-done.2 = f32[8,1,512]{2,1,0:T(1,128)S(1)} async-done(((f32[8,1,512]{2,1,0:T(1,128)}), f32[8,1,512]{2,1,0:T(1,128)S(1)}, u32[]{:S(2)}, u32[]{:S(2)}) %all-to-all-start.2) | async-done | bytes 16416 | tf_op jit(solution)/shard_map/all_to_all | solution.py:96
  60.1 0.8 reshape.127
  62.1 3.3 %all-to-all-start.3 = ((f32[4,1,1024]{2,1,0:T(1,128)}), f32[4,1,1024]{2,1,0:T(1,128)S(1)}, u32[]{:S(2)}, u32[]{:S(2)}) async-start(f32[4,1,1024]{2,1,0:T(1,128)} %reshape.128), calls=%async_computation.3 | async-start | bytes 32768 | tf_op jit(solution)/shard_map/all_to_all | solution.py:101
  65.4 3.7 %all-to-all-done.3 = f32[4,1,1024]{2,1,0:T(1,128)S(1)} async-done(((f32[4,1,1024]{2,1,0:T(1,128)}), f32[4,1,1024]{2,1,0:T(1,128)S(1)}, u32[]{:S(2)}, u32[]{:S(2)}) %all-to-all-start.3) | async-done | bytes 16416 | tf_op jit(solution)/shard_map/all_to_all | solution.py:101
  74.1 3.3 %all-to-all-start.5 = ((f32[4,1,1024]{2,1,0:T(1,128)}), f32[4,1,1024]{2,1,0:T(1,128)S(1)}, u32[]{:S(2)}, u32[]{:S(2)}) async-start(f32[4,1,1024]{2,1,0:T(1,128)} %reshape.130), calls=%async_computation.5 | async-start | bytes 32768 | tf_op jit(solution)/shard_map/all_to_all | solution.py:107
  77.4 3.8 %all-to-all-done.5 = f32[4,1,1024]{2,1,0:T(1,128)S(1)} async-done(((f32[4,1,1024]{2,1,0:T(1,128)}), f32[4,1,1024]{2,1,0:T(1,128)S(1)}, u32[]{:S(2)}, u32[]{:S(2)}) %all-to-all-start.5) | async-done | bytes 16416 | tf_op jit(solution)/shard_map/all_to_all | solution.py:107
  82.2 1.0 copy.77
  83.3 30.8 %all-gather = f32[2,1,512]{0,2,1:T(8,128)S(1)} all-gather(f32[2,1,64]{0,2,1:T(8,128)S(1)} %slice.1420), channel_id=2, replica_groups=mesh['lon'=8,'lat'=4] {'lon'}, dimensions={2}, use_global_device_ids=true | all-gather | bytes 4608 | tf_op jit(solution)/shard_map/all_gather | solution.py:117
  115.7 30.7 %all-gather.1 = f32[2,1,512]{0,2,1:T(8,128)S(1)} all-gather(f32[2,1,64]{0,2,1:T(8,128)S(1)} %slice.1421), channel_id=3, replica_groups=mesh['lon'=8,'lat'=4] {'lon'}, dimensions={2}, use_global_device_ids=true | all-gather | bytes 4608 | tf_op jit(solution)/shard_map/all_gather | solution.py:117
  147.9 6.2 %all_to_all.168 = f32[4,1,1024]{2,1,0:T(1,128)S(1)} all-to-all(f32[4,1,1024]{2,1,0:T(1,128)S(1)} %reshape.132), channel_id=1, replica_groups=mesh['lon'=8,'lat'=4] {'lat'}, dimensions={0} | all-to-all | bytes 32768 | tf_op jit(solution)/shard_map/all_to_all | solution.py:101
  156.5 6.2 %all_to_all.169 = f32[4,1,1024]{2,1,0:T(1,128)S(1)} all-to-all(f32[4,1,1024]{2,1,0:T(1,128)S(1)} %reshape.134), channel_id=1, replica_groups=mesh['lon'=8,'lat'=4] {'lat'}, dimensions={0} | all-to-all | bytes 32768 | tf_op jit(solution)/shard_map/all_to_all | solution.py:107
  164.0 8.9 %all_to_all.170 = f32[8,1,512]{2,1,0:T(1,128)S(1)} all-to-all(f32[8,1,512]{2,1,0:T(1,128)S(1)} %reshape.136), channel_id=1, replica_groups=mesh['lon'=8,'lat'=4] {'lon'}, dimensions={0} | all-to-all | bytes 32768 | tf_op jit(solution)/shard_map/all_to_all | solution.py:95
  176.6 8.9 %all_to_all.171 = f32[8,1,512]{2,1,0:T(1,128)S(1)} all-to-all(f32[8,1,512]{2,1,0:T(1,128)S(1)} %reshape.138), channel_id=1, replica_groups=mesh['lon'=8,'lat'=4] {'lon'}, dimensions={0} | all-to-all | bytes 32768 | tf_op jit(solution)/shard_map/all_to_all | solution.py:96
  186.3 0.8 reshape.139
  (269 shorter events, 34.3 us)
Async XLA Ops:
  0.7 7.5 %copy-start.6 = (s32[64]{0:T(128)S(1)}, s32[64]{0:T(128)}, u32[]{:S(2)}) copy-start(s32[64]{0:T(128)} %param.19) | copy-start | bytes 772
  0.7 9.2 %collective-permute-start.1 = (f32[1,64]{1,0:T(1,128)S(1)}, f32[1,64]{1,0:T(1,128)S(1)}, u32[]{:S(2)}, u32[]{:S(2)}) collective-permute-start(f32[1,64]{1,0:T(1,128)S(1)} %slice.1367), channel_id=1, source_target_pairs={{1,0},{2,1},{3,2},{5,4},{6,5},{7,6},{9,8},{10,9},{11,10},{13,12},{... | collective-permute-start | bytes 776 | tf_op jit(solution)/shard_map/ppermute | solution.py:16
  2.1 7.7 %collective-permute-start = (f32[32,1]{1,0:T(8,128)S(1)}, f32[32,1]{1,0:T(8,128)S(1)}, u32[]{:S(2)}, u32[]{:S(2)}) collective-permute-start(f32[32,1]{1,0:T(8,128)S(1)} %bitcast.116), channel_id=1, source_target_pairs={{4,0},{8,4},{12,8},{16,12},{20,16},{24,20},{28,24},{0,28},{5,1},{9... | collective-permute-start | bytes 392 | tf_op jit(solution)/shard_map/ppermute | solution.py:10
  8.2 0.8 copy-start
  8.2 0.8 copy-start.2
  9.0 0.8 copy-start.3
  9.8 0.7 copy-start.1
  11.4 3.6 %copy-start.4 = (f32[2,32,64]{2,1,0:T(8,128)S(1)}, f32[2,32,64]{2,1,0:T(8,128)}, u32[]{:S(2)}) copy-start(f32[2,32,64]{2,1,0:T(8,128)} %param.15) | copy-start | bytes 49156
  11.4 7.4 %all-to-all-start.4 = ((f32[4,1,1024]{2,1,0:T(1,128)}), f32[4,1,1024]{2,1,0:T(1,128)S(1)}, u32[]{:S(2)}, u32[]{:S(2)}) async-start(f32[4,1,1024]{2,1,0:T(1,128)} %reshape.120), calls=%async_computation.4 | async-start | bytes 32768 | tf_op jit(solution)/shard_map/all_to_all | solution.py:90
  18.8 12.0 %all-to-all-start = ((f32[8,1,512]{2,1,0:T(1,128)}), f32[8,1,512]{2,1,0:T(1,128)S(1)}, u32[]{:S(2)}, u32[]{:S(2)}) async-start(f32[8,1,512]{2,1,0:T(1,128)} %reshape.122), calls=%async_computation | async-start | bytes 32768 | tf_op jit(solution)/shard_map/all_to_all | solution.py:95
  30.8 9.9 %all-to-all-start.1 = ((f32[8,1,512]{2,1,0:T(1,128)}), f32[8,1,512]{2,1,0:T(1,128)S(1)}, u32[]{:S(2)}, u32[]{:S(2)}) async-start(f32[8,1,512]{2,1,0:T(1,128)} %reshape.124), calls=%async_computation.1 | async-start | bytes 32768 | tf_op jit(solution)/shard_map/all_to_all | solution.py:89
  49.5 9.9 %all-to-all-start.2 = ((f32[8,1,512]{2,1,0:T(1,128)}), f32[8,1,512]{2,1,0:T(1,128)S(1)}, u32[]{:S(2)}, u32[]{:S(2)}) async-start(f32[8,1,512]{2,1,0:T(1,128)} %reshape.126), calls=%async_computation.2 | async-start | bytes 32768 | tf_op jit(solution)/shard_map/all_to_all | solution.py:96
  62.1 7.1 %all-to-all-start.3 = ((f32[4,1,1024]{2,1,0:T(1,128)}), f32[4,1,1024]{2,1,0:T(1,128)S(1)}, u32[]{:S(2)}, u32[]{:S(2)}) async-start(f32[4,1,1024]{2,1,0:T(1,128)} %reshape.128), calls=%async_computation.3 | async-start | bytes 32768 | tf_op jit(solution)/shard_map/all_to_all | solution.py:101
  74.1 7.1 %all-to-all-start.5 = ((f32[4,1,1024]{2,1,0:T(1,128)}), f32[4,1,1024]{2,1,0:T(1,128)S(1)}, u32[]{:S(2)}, u32[]{:S(2)}) async-start(f32[4,1,1024]{2,1,0:T(1,128)} %reshape.130), calls=%async_computation.5 | async-start | bytes 32768 | tf_op jit(solution)/shard_map/all_to_all | solution.py:107
  114.7 0.7 copy-start.5
where the time goes:
time: 189 us; the launch traced here: 188 us
  blocking collectives  91.9 us (49%)
  starting transfers between devices  29.6 us (16%)
  waiting for transfers between devices  27.5 us (15%)
  local copies, waits for them, and re-layouts  24.2 us (13%)
  other arithmetic  14 us (7%)
    all_gather x2, blocking collectives, fold_natural(): whole_row = lax.all_gather(top_cells, 'lon', axis=1, tiled=True)  61.6 us
    unnamed x35, local copies, waits for them, and re-layouts  10.7 us
    all_to_all x1, blocking collectives, zonal_pass(): lax.all_to_all(current, 'lon', split_axis=1, concat_axis=2, tiled=True)  8.94 us
    all_to_all x1, blocking collectives, zonal_pass(): lax.all_to_all(cyclic_solve(zonal_lines, lines), 'lon', split_axis=2, con...  8.94 us
    all_to_all x1, waiting for transfers between devices, zonal_pass(): lax.all_to_all(cyclic_solve(zonal_lines, lines), 'lon', split_axis=2, con...  6.44 us
    all_to_all x1, blocking collectives, merid_open(): lax.all_to_all(to_columns(current, lanes), 'lat', split_axis=0, concat_ax...  6.21 us
    all_to_all x1, blocking collectives, merid_close(): lax.all_to_all(columns[None], 'lat', split_axis=3, concat_axis=0, tiled=T...  6.21 us
    ppermute x1, starting transfers between devices, passed_along(): return lax.ppermute(block, axis, route)  6.03 us
  transfers between devices with their start and end apart: 8, of which 6 were waited for; matrix products, arithmetic and copies ran while one was open for 2% of the time, Pallas kernels for 0%

commit v1 on v0

--- a/solution.py
+++ b/solution.py
@@ -2,6 +2,23 @@
 import jax.numpy as jnp
 from jax import lax
 from jax.sharding import PartitionSpec as P
+
+
+def laid_out(blocks, dim):
+    blocks = jnp.moveaxis(blocks, 0, dim)
+    shape = blocks.shape
+    return blocks.reshape(*shape[:dim], shape[dim] * shape[dim + 1], *shape[dim + 2 :])
+
+
+def grow_blocks(shard, axis):
+    length, here = (lax.axis_size(axis), lax.axis_index(axis))
+    pieces, apart = (shard[None], 1)
+    while apart < length:
+        other = lax.ppermute(pieces, axis, [(i, i ^ apart) for i in range(length)])
+        low = here & apart == 0
+        pieces = jnp.concatenate([jnp.where(low, pieces, other), jnp.where(low, other, pieces)])
+        apart *= 2
+    return pieces
 
 
 def passed_along(block, axis, distance):
@@ -114,7 +131,7 @@
 
     def fold_natural(values):
         top_cells = values[:, -1, :]
-        whole_row = lax.all_gather(top_cells, "lon", axis=1, tiled=True)
+        whole_row = laid_out(grow_blocks(top_cells, "lon"), 1)
         partner = jnp.take(whole_row, fold_pair, axis=1)
         return values.at[:, -1, :].set(jnp.where(is_top, 0.5 * (top_cells + partner), top_cells))
 

time: 189 us -> 151 us (0.80)
  blocking collectives: 91.9 us -> 30.3 us
  waiting for transfers between devices: 27.5 us -> 47.3 us
  starting transfers between devices: 29.6 us -> 33.7 us
    all_gather x2 -> x0, blocking collectives: 61.6 us -> none  [fold_natural(): whole_row = lax.all_gather(top_cells, 'lon', axis=1, tiled=True)]
    ppermute x0 -> x6, waiting for transfers between devices: none -> 19.2 us  [grow_blocks(): other = lax.ppermute(pieces, axis, [(i, i ^ apart) for i in range(length)])]
    ppermute x0 -> x6, starting transfers between devices: none -> 3.46 us  [grow_blocks(): other = lax.ppermute(pieces, axis, [(i, i ^ apart) for i in range(length)])]
    unnamed x35 -> x36, local copies, waits for them, and re-layouts: 10.7 us -> 9.05 us
  transfers between devices with their start and end apart: 8 -> 14, of which waited for: 6 -> 13; matrix products, arithmetic and copies ran while one was open for 2% -> 4% of each run, Pallas kernels for 0% -> 0%
where the time goes in v1:
time: 151 us; the launch traced here: 150 us
  waiting for transfers between devices  47.3 us (31%)
  starting transfers between devices  33.7 us (22%)
  blocking collectives  30.3 us (20%)
  local copies, waits for them, and re-layouts  24.2 us (16%)
  other arithmetic  13.2 us (9%)
    ppermute x6, waiting for transfers between devices, grow_blocks(): other = lax.ppermute(pieces, axis, [(i, i ^ apart) for i in range(length)])  19.2 us
    unnamed x36, local copies, waits for them, and re-layouts  9.05 us
    all_to_all x1, blocking collectives, zonal_pass(): lax.all_to_all(current, 'lon', split_axis=1, concat_axis=2, tiled=True)  8.94 us
    all_to_all x1, blocking collectives, zonal_pass(): lax.all_to_all(cyclic_solve(zonal_lines, lines), 'lon', split_axis=2, con...  8.94 us
    all_to_all x1, waiting for transfers between devices, zonal_pass(): lax.all_to_all(cyclic_solve(zonal_lines, lines), 'lon', split_axis=2, con...  6.44 us
    all_to_all x1, blocking collectives, merid_close(): lax.all_to_all(columns[None], 'lat', split_axis=3, concat_axis=0, tiled=T...  6.21 us
    all_to_all x1, blocking collectives, merid_open(): lax.all_to_all(to_columns(current, lanes), 'lat', split_axis=0, concat_ax...  6.21 us
    all_to_all x1, starting transfers between devices, zonal_pass(): lax.all_to_all(current, 'lon', split_axis=1, concat_axis=2, tiled=True)  6.11 us
  transfers between devices with their start and end apart: 14, of which 13 were waited for; matrix products, arithmetic and copies ran while one was open for 4% of the time, Pallas kernels for 0%

profile of v1, /device:TPU:0, one launch (start us, length us, event | category | flops | bytes accessed | tf_op | source)
XLA Modules:
  0.0 149.5 jit_solution(2747146416814963600)
XLA Ops:
  2.0 6.0 %collective-permute-start = (f32[32,1]{1,0:T(8,128)S(1)}, f32[32,1]{1,0:T(8,128)S(1)}, u32[]{:S(2)}, u32[]{:S(2)}) collective-permute-start(f32[32,1]{1,0:T(8,128)S(1)} %bitcast.127), channel_id=1, source_target_pairs={{4,0},{8,4},{12,8},{16,12},{20,16},{24,20},{28,24},{0,28},{5,1},{9... | collective-permute-start | bytes 392 | tf_op jit(solution)/shard_map/ppermute | solution.py:27
  10.6 3.5 %all-to-all-start.4 = ((f32[4,1,1024]{2,1,0:T(1,128)}), f32[4,1,1024]{2,1,0:T(1,128)S(1)}, u32[]{:S(2)}, u32[]{:S(2)}) async-start(f32[4,1,1024]{2,1,0:T(1,128)} %reshape.128), calls=%async_computation.4 | async-start | bytes 32768 | tf_op jit(solution)/shard_map/all_to_all | solution.py:107
  14.8 3.1 %all-to-all-done.4 = f32[4,1,1024]{2,1,0:T(1,128)S(1)} async-done(((f32[4,1,1024]{2,1,0:T(1,128)}), f32[4,1,1024]{2,1,0:T(1,128)S(1)}, u32[]{:S(2)}, u32[]{:S(2)}) %all-to-all-start.4) | async-done | bytes 16416 | tf_op jit(solution)/shard_map/all_to_all | solution.py:107
  18.0 6.1 %all-to-all-start = ((f32[8,1,512]{2,1,0:T(1,128)}), f32[8,1,512]{2,1,0:T(1,128)S(1)}, u32[]{:S(2)}, u32[]{:S(2)}) async-start(f32[8,1,512]{2,1,0:T(1,128)} %reshape.130), calls=%async_computation | async-start | bytes 32768 | tf_op jit(solution)/shard_map/all_to_all | solution.py:112
  25.6 5.0 %all-to-all-done = f32[8,1,512]{2,1,0:T(1,128)S(1)} async-done(((f32[8,1,512]{2,1,0:T(1,128)}), f32[8,1,512]{2,1,0:T(1,128)S(1)}, u32[]{:S(2)}, u32[]{:S(2)}) %all-to-all-start) | async-done | bytes 16416 | tf_op jit(solution)/shard_map/all_to_all | solution.py:112
  30.7 3.3 %all-to-all-start.1 = ((f32[8,1,512]{2,1,0:T(1,128)}), f32[8,1,512]{2,1,0:T(1,128)S(1)}, u32[]{:S(2)}, u32[]{:S(2)}) async-start(f32[8,1,512]{2,1,0:T(1,128)} %reshape.132), calls=%async_computation.1 | async-start | bytes 32768 | tf_op jit(solution)/shard_map/all_to_all | solution.py:106
  35.0 5.5 %all-to-all-done.1 = f32[8,1,512]{2,1,0:T(1,128)S(1)} async-done(((f32[8,1,512]{2,1,0:T(1,128)}), f32[8,1,512]{2,1,0:T(1,128)S(1)}, u32[]{:S(2)}, u32[]{:S(2)}) %all-to-all-start.1) | async-done | bytes 16416 | tf_op jit(solution)/shard_map/all_to_all | solution.py:106
  48.0 1.3 reshape.134
  49.3 3.3 %all-to-all-start.2 = ((f32[8,1,512]{2,1,0:T(1,128)}), f32[8,1,512]{2,1,0:T(1,128)S(1)}, u32[]{:S(2)}, u32[]{:S(2)}) async-start(f32[8,1,512]{2,1,0:T(1,128)} %reshape.134), calls=%async_computation.2 | async-start | bytes 32768 | tf_op jit(solution)/shard_map/all_to_all | solution.py:113
  52.7 6.4 %all-to-all-done.2 = f32[8,1,512]{2,1,0:T(1,128)S(1)} async-done(((f32[8,1,512]{2,1,0:T(1,128)}), f32[8,1,512]{2,1,0:T(1,128)S(1)}, u32[]{:S(2)}, u32[]{:S(2)}) %all-to-all-start.2) | async-done | bytes 16416 | tf_op jit(solution)/shard_map/all_to_all | solution.py:113
  61.9 3.3 %all-to-all-start.3 = ((f32[4,1,1024]{2,1,0:T(1,128)}), f32[4,1,1024]{2,1,0:T(1,128)S(1)}, u32[]{:S(2)}, u32[]{:S(2)}) async-start(f32[4,1,1024]{2,1,0:T(1,128)} %reshape.136), calls=%async_computation.3 | async-start | bytes 32768 | tf_op jit(solution)/shard_map/all_to_all | solution.py:118
  65.2 3.7 %all-to-all-done.3 = f32[4,1,1024]{2,1,0:T(1,128)S(1)} async-done(((f32[4,1,1024]{2,1,0:T(1,128)}), f32[4,1,1024]{2,1,0:T(1,128)S(1)}, u32[]{:S(2)}, u32[]{:S(2)}) %all-to-all-start.3) | async-done | bytes 16416 | tf_op jit(solution)/shard_map/all_to_all | solution.py:118
  73.8 3.4 %all-to-all-start.5 = ((f32[4,1,1024]{2,1,0:T(1,128)}), f32[4,1,1024]{2,1,0:T(1,128)S(1)}, u32[]{:S(2)}, u32[]{:S(2)}) async-start(f32[4,1,1024]{2,1,0:T(1,128)} %reshape.138), calls=%async_computation.5 | async-start | bytes 32768 | tf_op jit(solution)/shard_map/all_to_all | solution.py:124
  77.2 3.8 %all-to-all-done.5 = f32[4,1,1024]{2,1,0:T(1,128)S(1)} async-done(((f32[4,1,1024]{2,1,0:T(1,128)}), f32[4,1,1024]{2,1,0:T(1,128)S(1)}, u32[]{:S(2)}, u32[]{:S(2)}) %all-to-all-start.5) | async-done | bytes 16416 | tf_op jit(solution)/shard_map/all_to_all | solution.py:124
  82.8 3.0 %collective-permute-done.2 = f32[1,2,64]{2,1,0:T(2,128)S(1)} collective-permute-done((f32[1,2,64]{2,1,0:T(2,128)S(1)}, f32[1,2,64]{2,1,0:T(2,128)S(1)}, u32[]{:S(2)}, u32[]{:S(2)}) %collective-permute-start.2) | collective-permute-done | bytes 544 | tf_op jit(solution)/shard_map/ppermute | solution.py:17
  86.4 3.1 %collective-permute-done.3 = f32[2,2,64]{2,1,0:T(2,128)S(1)} collective-permute-done((f32[2,2,64]{2,1,0:T(2,128)S(1)}, f32[2,2,64]{2,1,0:T(2,128)S(1)}, u32[]{:S(2)}, u32[]{:S(2)}) %collective-permute-start.3) | collective-permute-done | bytes 1056 | tf_op jit(solution)/shard_map/ppermute | solution.py:17
  90.7 3.4 %collective-permute-done.4 = f32[4,2,64]{2,1,0:T(2,128)S(1)} collective-permute-done((f32[4,2,64]{2,1,0:T(2,128)S(1)}, f32[4,2,64]{2,1,0:T(2,128)S(1)}, u32[]{:S(2)}, u32[]{:S(2)}) %collective-permute-start.4) | collective-permute-done | bytes 2080 | tf_op jit(solution)/shard_map/ppermute | solution.py:17
  96.6 3.0 %collective-permute-done.5 = f32[1,2,64]{2,1,0:T(2,128)S(1)} collective-permute-done((f32[1,2,64]{2,1,0:T(2,128)S(1)}, f32[1,2,64]{2,1,0:T(2,128)S(1)}, u32[]{:S(2)}, u32[]{:S(2)}) %collective-permute-start.5) | collective-permute-done | bytes 544 | tf_op jit(solution)/shard_map/ppermute | solution.py:17
  100.2 3.1 %collective-permute-done.6 = f32[2,2,64]{2,1,0:T(2,128)S(1)} collective-permute-done((f32[2,2,64]{2,1,0:T(2,128)S(1)}, f32[2,2,64]{2,1,0:T(2,128)S(1)}, u32[]{:S(2)}, u32[]{:S(2)}) %collective-permute-start.6) | collective-permute-done | bytes 1056 | tf_op jit(solution)/shard_map/ppermute | solution.py:17
  104.4 3.5 %collective-permute-done.7 = f32[4,2,64]{2,1,0:T(2,128)S(1)} collective-permute-done((f32[4,2,64]{2,1,0:T(2,128)S(1)}, f32[4,2,64]{2,1,0:T(2,128)S(1)}, u32[]{:S(2)}, u32[]{:S(2)}) %collective-permute-start.7) | collective-permute-done | bytes 2080 | tf_op jit(solution)/shard_map/ppermute | solution.py:17
  109.7 6.2 %all_to_all.168 = f32[4,1,1024]{2,1,0:T(1,128)S(1)} all-to-all(f32[4,1,1024]{2,1,0:T(1,128)S(1)} %reshape.140), channel_id=1, replica_groups=mesh['lon'=8,'lat'=4] {'lat'}, dimensions={0} | all-to-all | bytes 32768 | tf_op jit(solution)/shard_map/all_to_all | solution.py:118
  118.2 6.2 %all_to_all.169 = f32[4,1,1024]{2,1,0:T(1,128)S(1)} all-to-all(f32[4,1,1024]{2,1,0:T(1,128)S(1)} %reshape.142), channel_id=1, replica_groups=mesh['lon'=8,'lat'=4] {'lat'}, dimensions={0} | all-to-all | bytes 32768 | tf_op jit(solution)/shard_map/all_to_all | solution.py:124
  125.6 8.9 %all_to_all.170 = f32[8,1,512]{2,1,0:T(1,128)S(1)} all-to-all(f32[8,1,512]{2,1,0:T(1,128)S(1)} %reshape.144), channel_id=1, replica_groups=mesh['lon'=8,'lat'=4] {'lon'}, dimensions={0} | all-to-all | bytes 32768 | tf_op jit(solution)/shard_map/all_to_all | solution.py:112
  138.2 8.9 %all_to_all.171 = f32[8,1,512]{2,1,0:T(1,128)S(1)} all-to-all(f32[8,1,512]{2,1,0:T(1,128)S(1)} %reshape.146), channel_id=1, replica_groups=mesh['lon'=8,'lat'=4] {'lon'}, dimensions={0} | all-to-all | bytes 32768 | tf_op jit(solution)/shard_map/all_to_all | solution.py:113
  (300 shorter events, 41.3 us)
Async XLA Ops:
  0.7 8.8 %collective-permute-start.1 = (f32[1,64]{1,0:T(1,128)S(1)}, f32[1,64]{1,0:T(1,128)S(1)}, u32[]{:S(2)}, u32[]{:S(2)}) collective-permute-start(f32[1,64]{1,0:T(1,128)S(1)} %slice.1367), channel_id=1, source_target_pairs={{1,0},{2,1},{3,2},{5,4},{6,5},{7,6},{9,8},{10,9},{11,10},{13,12},{... | collective-permute-start | bytes 776 | tf_op jit(solution)/shard_map/ppermute | solution.py:33
  2.0 6.1 %copy-start = (f32[2,32,64]{2,1,0:T(8,128)S(1)}, f32[2,32,64]{2,1,0:T(8,128)}, u32[]{:S(2)}) copy-start(f32[2,32,64]{2,1,0:T(8,128)} %param.14) | copy-start | bytes 49156
  2.0 6.1 %copy-start.2 = (f32[2,32,64]{2,1,0:T(8,128)S(1)}, f32[2,32,64]{2,1,0:T(8,128)}, u32[]{:S(2)}) copy-start(f32[2,32,64]{2,1,0:T(8,128)} %param.13) | copy-start | bytes 49156
  2.0 7.5 %collective-permute-start = (f32[32,1]{1,0:T(8,128)S(1)}, f32[32,1]{1,0:T(8,128)S(1)}, u32[]{:S(2)}, u32[]{:S(2)}) collective-permute-start(f32[32,1]{1,0:T(8,128)S(1)} %bitcast.127), channel_id=1, source_target_pairs={{4,0},{8,4},{12,8},{16,12},{20,16},{24,20},{28,24},{0,28},{5,1},{9... | collective-permute-start | bytes 392 | tf_op jit(solution)/shard_map/ppermute | solution.py:27
  8.2 0.8 copy-start.3
  9.0 0.7 copy-start.1
  10.6 3.6 %copy-start.4 = (f32[2,32,64]{2,1,0:T(8,128)S(1)}, f32[2,32,64]{2,1,0:T(8,128)}, u32[]{:S(2)}) copy-start(f32[2,32,64]{2,1,0:T(8,128)} %param.15) | copy-start | bytes 49156
  10.6 7.4 %all-to-all-start.4 = ((f32[4,1,1024]{2,1,0:T(1,128)}), f32[4,1,1024]{2,1,0:T(1,128)S(1)}, u32[]{:S(2)}, u32[]{:S(2)}) async-start(f32[4,1,1024]{2,1,0:T(1,128)} %reshape.128), calls=%async_computation.4 | async-start | bytes 32768 | tf_op jit(solution)/shard_map/all_to_all | solution.py:107
  18.0 12.7 %all-to-all-start = ((f32[8,1,512]{2,1,0:T(1,128)}), f32[8,1,512]{2,1,0:T(1,128)S(1)}, u32[]{:S(2)}, u32[]{:S(2)}) async-start(f32[8,1,512]{2,1,0:T(1,128)} %reshape.130), calls=%async_computation | async-start | bytes 32768 | tf_op jit(solution)/shard_map/all_to_all | solution.py:112
  30.7 9.9 %all-to-all-start.1 = ((f32[8,1,512]{2,1,0:T(1,128)}), f32[8,1,512]{2,1,0:T(1,128)S(1)}, u32[]{:S(2)}, u32[]{:S(2)}) async-start(f32[8,1,512]{2,1,0:T(1,128)} %reshape.132), calls=%async_computation.1 | async-start | bytes 32768 | tf_op jit(solution)/shard_map/all_to_all | solution.py:106
  49.3 9.9 %all-to-all-start.2 = ((f32[8,1,512]{2,1,0:T(1,128)}), f32[8,1,512]{2,1,0:T(1,128)S(1)}, u32[]{:S(2)}, u32[]{:S(2)}) async-start(f32[8,1,512]{2,1,0:T(1,128)} %reshape.134), calls=%async_computation.2 | async-start | bytes 32768 | tf_op jit(solution)/shard_map/all_to_all | solution.py:113
  61.9 7.1 %all-to-all-start.3 = ((f32[4,1,1024]{2,1,0:T(1,128)}), f32[4,1,1024]{2,1,0:T(1,128)S(1)}, u32[]{:S(2)}, u32[]{:S(2)}) async-start(f32[4,1,1024]{2,1,0:T(1,128)} %reshape.136), calls=%async_computation.3 | async-start | bytes 32768 | tf_op jit(solution)/shard_map/all_to_all | solution.py:118
  73.8 3.4 %copy-start.6 = (s32[64]{0:T(128)S(1)}, s32[64]{0:T(128)}, u32[]{:S(2)}) copy-start(s32[64]{0:T(128)} %param.19) | copy-start | bytes 772
  73.8 7.2 %all-to-all-start.5 = ((f32[4,1,1024]{2,1,0:T(1,128)}), f32[4,1,1024]{2,1,0:T(1,128)S(1)}, u32[]{:S(2)}, u32[]{:S(2)}) async-start(f32[4,1,1024]{2,1,0:T(1,128)} %reshape.138), calls=%async_computation.5 | async-start | bytes 32768 | tf_op jit(solution)/shard_map/all_to_all | solution.py:124
  82.2 3.6 %collective-permute-start.2 = (f32[1,2,64]{2,1,0:T(2,128)S(1)}, f32[1,2,64]{2,1,0:T(2,128)S(1)}, u32[]{:S(2)}, u32[]{:S(2)}) collective-permute-start(f32[1,2,64]{2,1,0:T(2,128)S(1)} %bitcast.149), channel_id=1, source_target_pairs={{0,4},{4,0},{8,12},{12,8},{16,20},{20,16},{24,28},{28,24},{1,5},{5... | collective-permute-start | bytes 1544 | tf_op jit(solution)/shard_map/ppermute | solution.py:17
  85.9 3.6 %collective-permute-start.3 = (f32[2,2,64]{2,1,0:T(2,128)S(1)}, f32[2,2,64]{2,1,0:T(2,128)S(1)}, u32[]{:S(2)}, u32[]{:S(2)}) collective-permute-start(f32[2,2,64]{2,1,0:T(2,128)S(1)} %pad_maximum_fusion.8), channel_id=1, source_target_pairs={{0,8},{4,12},{8,0},{12,4},{16,24},{20,28},{24,16},{28,20},{1,9},{5... | collective-permute-start | bytes 3080 | tf_op jit(solution)/shard_map/ppermute | solution.py:17
  86.4 3.7 %copy-start.5 = (f32[32,64]{1,0:T(8,128)S(1)}, f32[32,64]{1,0:T(8,128)}, u32[]{:S(2)}) copy-start(f32[32,64]{1,0:T(8,128)} %param.17) | copy-start | bytes 24580
  89.5 4.6 %collective-permute-start.4 = (f32[4,2,64]{2,1,0:T(2,128)S(1)}, f32[4,2,64]{2,1,0:T(2,128)S(1)}, u32[]{:S(2)}, u32[]{:S(2)}) collective-permute-start(f32[4,2,64]{2,1,0:T(2,128)S(1)} %pad_maximum_fusion.6), channel_id=1, source_target_pairs={{0,16},{4,20},{8,24},{12,28},{16,0},{20,4},{24,8},{28,12},{1,17},{... | collective-permute-start | bytes 6152 | tf_op jit(solution)/shard_map/ppermute | solution.py:17
  96.0 3.6 %collective-permute-start.5 = (f32[1,2,64]{2,1,0:T(2,128)S(1)}, f32[1,2,64]{2,1,0:T(2,128)S(1)}, u32[]{:S(2)}, u32[]{:S(2)}) collective-permute-start(f32[1,2,64]{2,1,0:T(2,128)S(1)} %bitcast.150), channel_id=1, source_target_pairs={{0,4},{4,0},{8,12},{12,8},{16,20},{20,16},{24,28},{28,24},{1,5},{5... | collective-permute-start | bytes 1544 | tf_op jit(solution)/shard_map/ppermute | solution.py:17
  99.6 3.6 %collective-permute-start.6 = (f32[2,2,64]{2,1,0:T(2,128)S(1)}, f32[2,2,64]{2,1,0:T(2,128)S(1)}, u32[]{:S(2)}, u32[]{:S(2)}) collective-permute-start(f32[2,2,64]{2,1,0:T(2,128)S(1)} %pad_maximum_fusion.9), channel_id=1, source_target_pairs={{0,8},{4,12},{8,0},{12,4},{16,24},{20,28},{24,16},{28,20},{1,9},{5... | collective-permute-start | bytes 3080 | tf_op jit(solution)/shard_map/ppermute | solution.py:17
  103.3 4.6 %collective-permute-start.7 = (f32[4,2,64]{2,1,0:T(2,128)S(1)}, f32[4,2,64]{2,1,0:T(2,128)S(1)}, u32[]{:S(2)}, u32[]{:S(2)}) collective-permute-start(f32[4,2,64]{2,1,0:T(2,128)S(1)} %pad_maximum_fusion.7), channel_id=1, source_target_pairs={{0,16},{4,20},{8,24},{12,28},{16,0},{20,4},{24,8},{28,12},{1,17},{... | collective-permute-start | bytes 6152 | tf_op jit(solution)/shard_map/ppermute | solution.py:17
